TPU v7x, 32 devices: a whole 2x2x4 slice. The times are simulated.
32 devices in a mesh: row: 8 (over z, x), col: 4 (over y, core).
Axes of the slice: x: 2, y: 2, z: 4, core: 2. Of those that a mesh axis runs over, the one named last changes fastest.
Arguments:
- diag_inverse: bfloat16 [2, 8192, 8192], P(None, 'col', 'row'), as said below
- panel_rhs: bfloat16 [2, 8192, 128], P(None, 'row'), may hold values from -6 to 6
- below: bfloat16 [2, 22528, 8192], P(None, 'row', 'col'), may hold values from -0.03125 to 0.03125
- row_ids: int32 [2, 176], P(None, 'row'), may hold values from 0 to 256, as said below
- ancestor_rhs: bfloat16 [24576, 128], P(('row', 'col')), may hold values from -6 to 6
- ancestor_solution: bfloat16 [24576, 128], P(('row', 'col')), may hold values from -6 to 6
Outputs:
- solution: bfloat16 [2, 8192, 128], P(None, ('row', 'col'))
- rhs_updated: bfloat16 [24576, 128], P(('row', 'col'))
Inputs may be any that keep to these rules, and one draw needn't show every extreme that they name: diag_inverse[p] is lower triangular with a positive diagonal. `row_ids`: slots 22 r to 22 r + 21 of either panel belong to the r-th index of row. Each holds 256 (empty) or a later block row that this index owns: for panel 0 a panel-1 block row in [r * 8, r * 8 + 8) or a value in [64 + r * 24, 64 + r * 24 + 24); for panel 1 only the latter. Live ids of one panel are distinct. In each panel some index of row has all 22 slots live.
All inputs are finite; a program needn't handle non-finite values.
Results may differ from a plain program's by a relative error of at most 0.017.
Values may be sent and summed in bfloat16 or wider, within the bound.
A program may use at most 128 MiB of HBM per device.

v0:
```python
import jax
import jax.numpy as jnp
from jax import lax
from jax.sharding import PartitionSpec as P

BS = 128
NRHS = 128
PW = 64
CAP = 22
NA_R = 24


def on_device(diag_inverse, panel_rhs, below, row_ids, ancestor_rhs, ancestor_solution):
    row_count = lax.axis_size("row")
    row_place = lax.axis_index("row")
    col_place = lax.axis_index("col")
    panel_rows = PW // row_count
    contract_first = (((0,), (0,)), ((), ()))

    def row_total(partial_sum):
        return lax.psum(partial_sum.astype(jnp.bfloat16), "row").astype(jnp.float32)

    def col_total(partial_sum):
        return lax.psum(partial_sum.astype(jnp.bfloat16), "col").astype(jnp.float32)

    def pick_panel(slot_ids):
        position = slot_ids - row_place * panel_rows
        return (position[:, None] == jnp.arange(panel_rows)[None, :]) & (slot_ids[:, None] < PW)

    def pick_later(slot_ids):
        position = slot_ids - PW - row_place * NA_R
        return position[:, None] == jnp.arange(NA_R)[None, :]

    def to_rows(picked, slot_sums):
        placed = jnp.einsum(
            "sk,sbn->kbn", picked.astype(jnp.float32), slot_sums, precision=lax.Precision.HIGHEST
        )
        return placed.reshape(-1, NRHS)

    def slot_values(picked, source_rows):
        return jnp.einsum(
            "sk,kbn->sbn",
            picked.astype(jnp.bfloat16),
            source_rows,
            preferred_element_type=jnp.float32,
        )

    def transpose_product(panel_index, values):
        flat_values = values.astype(jnp.bfloat16).reshape(CAP * BS, NRHS)
        return lax.dot_general(
            below[panel_index], flat_values, contract_first, preferred_element_type=jnp.float32
        )

    def solve_back(forward_part, back_sum, panel_index):
        back_rhs = (forward_part.astype(jnp.float32) - back_sum).astype(jnp.bfloat16)
        return lax.dot_general(
            diag_inverse[panel_index], back_rhs, contract_first, preferred_element_type=jnp.float32
        )

    forward_zero = row_total(
        jnp.dot(diag_inverse[0], panel_rhs[0], preferred_element_type=jnp.float32)
    ).astype(jnp.bfloat16)
    slot_zero = jnp.dot(below[0], forward_zero, preferred_element_type=jnp.float32).reshape(
        CAP, BS, NRHS
    )
    panel_part = col_total(to_rows(pick_panel(row_ids[0]), slot_zero))
    panel_one_rhs = (panel_rhs[1].astype(jnp.float32) - panel_part).astype(jnp.bfloat16)
    forward_one = row_total(
        jnp.dot(diag_inverse[1], panel_one_rhs, preferred_element_type=jnp.float32)
    ).astype(jnp.bfloat16)
    later_zero = to_rows(pick_later(row_ids[0]), slot_zero)
    slot_one = jnp.dot(below[1], forward_one, preferred_element_type=jnp.float32).reshape(
        CAP, BS, NRHS
    )
    later_one = to_rows(pick_later(row_ids[1]), slot_one)

    def ancestor_share(partial_sum):
        return lax.psum_scatter(
            partial_sum.astype(jnp.bfloat16), "col", scatter_dimension=0, tiled=True
        ).astype(jnp.float32)

    update = ancestor_share(later_zero) + ancestor_share(later_one)
    rhs_updated = (ancestor_rhs.astype(jnp.float32) - update).astype(jnp.bfloat16)
    known_rows = lax.all_gather(ancestor_solution, "col", axis=0, tiled=True).reshape(
        NA_R, BS, NRHS
    )
    later_two = transpose_product(1, slot_values(pick_later(row_ids[1]), known_rows))
    ancestors_zero = slot_values(pick_later(row_ids[0]), known_rows)
    back_one = lax.psum(later_two.astype(jnp.bfloat16), "row").astype(jnp.float32)
    solution_one = col_total(solve_back(forward_one, back_one, 1)).astype(jnp.bfloat16)
    one_blocks = solution_one.reshape(panel_rows, BS, NRHS)
    values_zero = ancestors_zero + slot_values(pick_panel(row_ids[0]), one_blocks)
    back_zero = row_total(transpose_product(0, values_zero))
    share_rows = lax.psum_scatter(
        solve_back(forward_zero, back_zero, 0).astype(jnp.bfloat16),
        "col",
        scatter_dimension=0,
        tiled=True,
    )
    share_size = share_rows.shape[0]
    one_share = lax.dynamic_slice_in_dim(solution_one, col_place * share_size, share_size, 0)
    solution = jnp.stack([share_rows, one_share])
    return (solution, rhs_updated)


def solution(mesh):
    in_specs = (
        P(None, "col", "row"),
        P(None, "row", None),
        P(None, "row", "col"),
        P(None, "row"),
        P(("row", "col"), None),
        P(("row", "col"), None),
    )
    out_specs = (P(None, ("row", "col"), None), P(("row", "col"), None))
    return jax.shard_map(
        on_device, mesh=mesh, in_specs=in_specs, out_specs=out_specs, check_vma=False
    )
```

profile of v0, /device:TPU:0, one launch (start us, length us, event | category | flops | bytes accessed | tf_op | source)
XLA Modules:
  0.0 420.0 jit_solution(17048211158153917995)
XLA Ops:
  7.2 4.3 %fusion.30 = bf16[2048,128]{1,0:T(8,128)(2,1)} fusion(bf16[2,2048,1024]{2,1,0:T(8,128)(2,1)} %param.6, bf16[2,1024,128]{2,1,0:T(8,128)(2,1)} %param.7), kind=kOutput, calls=%fused_computation.26 | convolution fusion | flops 537133056 | bytes 4980736 | tf_op jit(solution)/shard_map/dot_general | solution.py:61
  11.6 10.1 %all_gather.3 = bf16[3072,128]{1,0:T(8,128)(2,1)S(1)} all-gather(bf16[768,128]{1,0:T(8,128)(2,1)S(1)} %copy-done.1), channel_id=1, replica_groups=mesh['row'=8,'col'=4] {'col'}, dimensions={0}, use_global_device_ids=true | all-gather | bytes 983040 | tf_op jit(solution)/shard_map/all_gather | solution.py:84
  22.6 64.5 %all-reduce.7.cloned.1.call-done = bf16[2048,128]{1,0:T(8,128)(2,1)} async-done(((bf16[2048,128]{1,0:T(8,128)(2,1)}), bf16[2048,128]{1,0:T(8,128)(2,1)}) %all-reduce.7.cloned.1.call-update) | async-done | bytes 524304 | tf_op jit(solution)/shard_map/psum | solution.py:21
  87.1 9.6 %fusion.20 = f32[2816,128]{0,1:T(8,128)} fusion(bf16[2048,128]{1,0:T(8,128)(2,1)} %all-reduce.7.cloned.1.call-done, bf16[2,2816,2048]{2,1,0:T(8,128)(2,1)} %param.8), kind=kOutput, calls=%fused_computation.20 | convolution fusion | flops 1476395008 | bytes 13500416 | tf_op jit(solution)/shard_map/dot_general | solution.py:63
  96.7 1.8 copy.17
  98.5 1.4 fusion.69
  100.7 6.8 %fusion.45 = bf16[2048,128]{0,1:T(8,128)(2,1)} fusion(bf16[2816,128]{1,0:T(8,128)(2,1)S(1)} %bitcast.120, bf16[2,2816,2048]{2,1,0:T(8,128)(2,1)} %param.8), kind=kOutput, calls=%fused_computation.31 | convolution fusion | flops 1476657152 | bytes 12779520 | tf_op jit(solution)/shard_map/dot_general | solution.py:50
  107.6 24.7 %all-reduce.9.cloned.1.call-done = bf16[1024,128]{1,0:T(8,128)(2,1)} async-done(((bf16[1024,128]{1,0:T(8,128)(2,1)}), bf16[1024,128]{1,0:T(8,128)(2,1)}) %all-reduce.9.cloned.1.call-update) | async-done | bytes 262160 | tf_op jit(solution)/shard_map/psum | solution.py:24
  132.3 4.6 %fusion.42 = bf16[2048,128]{0,1:T(8,128)(2,1)} fusion(bf16[2,2048,1024]{2,1,0:T(8,128)(2,1)} %param.6, bf16[1024,128]{1,0:T(8,128)(2,1)} %all-reduce.9.cloned.1.call-done, bf16[2,1024,128]{2,1,0:T(8,128)(2,1)S(1)} %copy-done.3), kind=kOutput, calls=%fused_computation.30 | convolution fusion | flops 537657344 | bytes 5242880 | tf_op jit(solution)/shard_map/dot_general | solution.py:69
  137.0 78.4 %all-reduce.15.cloned.1.call-done = (bf16[2048,128]{0,1:T(8,128)(2,1)}, bf16[2048,128]{0,1:T(8,128)(2,1)}) async-done(((bf16[2048,128]{0,1:T(8,128)(2,1)}, bf16[2048,128]{0,1:T(8,128)(2,1)}), (bf16[2048,128]{0,1:T(8,128)(2,1)}, bf16[2048,128]{0,1:T(8,128)(2,1)})) %all-reduce.15.cloned.1.call-update) | async-done | bytes 1048592 | tf_op jit(solution)/shard_map/psum | solution.py:89
  215.4 3.9 fusion.72
  219.6 31.8 %all-reduce.11.cloned.1.call-done = bf16[1024,128]{0,1:T(8,128)(2,1)} async-done(((bf16[1024,128]{0,1:T(8,128)(2,1)}), bf16[1024,128]{0,1:T(8,128)(2,1)}) %all-reduce.11.cloned.1.call-update) | async-done | bytes 262160 | tf_op jit(solution)/shard_map/psum | solution.py:24
  254.0 9.7 %fusion.48 = bf16[2048,128]{1,0:T(8,128)(2,1)} fusion(bf16[2816,128]{1,0:T(8,128)(2,1)S(1)} %bitcast.121, bf16[2,2816,2048]{2,1,0:T(8,128)(2,1)} %param.8), kind=kOutput, calls=%fused_computation.32 | convolution fusion | flops 1476657152 | bytes 12779520 | tf_op jit(solution)/shard_map/dot_general | solution.py:50
  263.8 72.8 %all-reduce.13.cloned.1.call-done = bf16[2048,128]{1,0:T(8,128)(2,1)} async-done(((bf16[2048,128]{1,0:T(8,128)(2,1)}), bf16[2048,128]{1,0:T(8,128)(2,1)}) %all-reduce.13.cloned.1.call-update) | async-done | bytes 524304 | tf_op jit(solution)/shard_map/psum | solution.py:21
  336.6 3.8 fusion.75
  340.5 1.6 fusion.57
  342.1 1.1 copy.26
  343.5 6.8 %fusion.23 = f32[2816,128]{0,1:T(8,128)S(1)} fusion(bf16[2048,128]{0,1:T(8,128)(2,1)} %get-tuple-element.7, bf16[2,2816,2048]{2,1,0:T(8,128)(2,1)} %param.8), kind=kOutput, calls=%fused_computation.21 | convolution fusion | flops 1476395008 | bytes 13500416 | tf_op jit(solution)/shard_map/dot_general | solution.py:72
  350.7 1.6 fusion.60
  352.3 1.1 copy.29
  354.3 5.5 %reduce-scatter.4.cloned.1.call-done = bf16[256,128]{0,1:T(8,128)(2,1)} async-done(((bf16[1024,128]{0,1:T(8,128)(2,1)}), bf16[256,128]{0,1:T(8,128)(2,1)}) %reduce-scatter.4.cloned.1.call-update) | async-done | bytes 65552 | tf_op jit(solution)/shard_map/reduce_scatter | solution.py:94
  361.4 24.2 %reduce-scatter.6.cloned.1.call-done = bf16[768,128]{1,0:T(8,128)(2,1)} async-done(((bf16[3072,128]{1,0:T(8,128)(2,1)}), bf16[768,128]{1,0:T(8,128)(2,1)}) %reduce-scatter.6.cloned.1.call-update) | async-done | bytes 196624 | tf_op jit(solution)/shard_map/reduce_scatter | solution.py:78
  385.6 25.8 %reduce-scatter.8.cloned.1.call-done = bf16[768,128]{1,0:T(8,128)(2,1)} async-done(((bf16[3072,128]{1,0:T(8,128)(2,1)}), bf16[768,128]{1,0:T(8,128)(2,1)}) %reduce-scatter.8.cloned.1.call-update) | async-done | bytes 196624 | tf_op jit(solution)/shard_map/reduce_scatter | solution.py:78
  411.3 1.8 subtract_convert_fusion.4
  (40 shorter events, 7.9 us)
Async XLA Ops:
  7.2 4.4 %copy-start.1 = (bf16[768,128]{1,0:T(8,128)(2,1)S(1)}, bf16[768,128]{1,0:T(8,128)(2,1)}, u32[]{:S(2)}) copy-start(bf16[768,128]{1,0:T(8,128)(2,1)} %param.11) | copy-start | bytes 589828
  7.2 14.6 %copy-start.2 = (s32[2,22]{1,0:T(2,128)S(1)}, s32[2,22]{1,0:T(2,128)}, u32[]{:S(2)}) copy-start(s32[2,22]{1,0:T(2,128)} %param.9) | copy-start | bytes 532
  7.2 79.9 %all-reduce.7.cloned.1.call-start = ((), (), s32[]{:S(2)}) async-start(), calls=%async_computation.3 | async-start | bytes 1048576 | tf_op jit(solution)/shard_map/psum | solution.py:21
  11.6 120.7 %all-reduce.9.cloned.1.call-start = ((), (), s32[]{:S(2)}) async-start(), calls=%async_computation.4 | async-start | bytes 524288 | tf_op jit(solution)/shard_map/psum | solution.py:24
  100.7 114.7 %all-reduce.15.cloned.1.call-start = ((), (), s32[]{:S(2)}) async-start(), calls=%async_computation.10 | async-start | bytes 2097152 | tf_op jit(solution)/shard_map/psum | solution.py:89
  100.7 31.6 %copy-start.3 = (bf16[2,1024,128]{2,1,0:T(8,128)(2,1)S(1)}, bf16[2,1024,128]{2,1,0:T(8,128)(2,1)}, u32[]{:S(2)}) copy-start(bf16[2,1024,128]{2,1,0:T(8,128)(2,1)} %param.7) | copy-start | bytes 1572868
  137.0 114.5 %all-reduce.11.cloned.1.call-start = ((), (), s32[]{:S(2)}) async-start(), calls=%async_computation.5 | async-start | bytes 524288 | tf_op jit(solution)/shard_map/psum | solution.py:24
  219.4 117.2 %all-reduce.13.cloned.1.call-start = ((), (), s32[]{:S(2)}) async-start(), calls=%async_computation.6 | async-start | bytes 1048576 | tf_op jit(solution)/shard_map/psum | solution.py:21
  254.0 82.6 %copy-start.4 = (bf16[2048,128]{1,0:T(8,128)(2,1)S(1)}, bf16[2048,128]{1,0:T(8,128)(2,1)}, u32[]{:S(2)}) copy-start(bf16[2048,128]{1,0:T(8,128)(2,1)} %all-reduce.7.cloned.1.call-done) | copy-start | bytes 1572868
  263.8 96.0 %reduce-scatter.4.cloned.1.call-start = ((), (), s32[]{:S(2)}) async-start(), calls=%async_computation.7 | async-start | bytes 327680 | tf_op jit(solution)/shard_map/reduce_scatter | solution.py:94
  340.4 45.1 %reduce-scatter.6.cloned.1.call-start = ((), (), s32[]{:S(2)}) async-start(), calls=%async_computation.8 | async-start | bytes 983040 | tf_op jit(solution)/shard_map/reduce_scatter | solution.py:78
  343.2 68.1 %reduce-scatter.8.cloned.1.call-start = ((), (), s32[]{:S(2)}) async-start(), calls=%async_computation.9 | async-start | bytes 983040 | tf_op jit(solution)/shard_map/reduce_scatter | solution.py:78
  350.3 61.1 %copy-start = (bf16[768,128]{1,0:T(8,128)(2,1)S(1)}, bf16[768,128]{1,0:T(8,128)(2,1)}, u32[]{:S(2)}) copy-start(bf16[768,128]{1,0:T(8,128)(2,1)} %param.10) | copy-start | bytes 589828
Sparse Core Ops, SparseCore 0:
  11.7 75.3 all-reduce.6
  100.8 31.4 all-reduce.8
  137.1 78.2 all-reduce.14
  219.5 31.9 all-reduce.10
  263.9 72.6 all-reduce.12
  340.5 19.2 reduce-scatter.3
  362.3 23.1 reduce-scatter.5
  388.1 23.1 reduce-scatter.7
where the time goes:
time: 420 us
  waiting for transfers between devices  328 us (78%)
  matrix products  56.1 us (13%)
  between operations  14.3 us (3%)
  blocking collectives  10.1 us (2%)
  local copies, waits for them, and re-layouts  8.26 us (2%)
    psum x2, waiting for transfers between devices, row_total(): return lax.psum(partial_sum.astype(jnp.bfloat16), 'row').astype(jnp.float32)  137 us
    psum x1, waiting for transfers between devices, on_device(): lax.psum(later_two.astype(jnp.bfloat16), 'row').astype(jnp.float32)  78.4 us
    psum x2, waiting for transfers between devices, col_total(): return lax.psum(partial_sum.astype(jnp.bfloat16), 'col').astype(jnp.float32)  56.6 us
    reduce_scatter x2, waiting for transfers between devices, ancestor_share(): lax.psum_scatter(partial_sum.astype(jnp.bfloat16), 'col', scatter_dimensi...  49.9 us
    dot_general x2, matrix products, transpose_product(): lax.dot_general(below[panel_index], flat_values, contract_first, preferre...  16.6 us
    all_gather x1, blocking collectives, on_device(): lax.all_gather(ancestor_solution, 'col', axis=0, tiled=True)  10.1 us
    dot_general x1, matrix products, on_device(): jnp.dot(below[0], forward_zero, preferred_element_type=jnp.float32)  9.59 us
  transfers between devices with their start and end apart: 8, of which 8 were waited for; matrix products, arithmetic and copies ran while one was open for 5% of the time, Pallas kernels for 0%

commit v1 on v0

--- a/solution.py
+++ b/solution.py
@@ -18,7 +18,9 @@
     contract_first = (((0,), (0,)), ((), ()))
 
     def row_total(partial_sum):
-        return lax.psum(partial_sum.astype(jnp.bfloat16), "row").astype(jnp.float32)
+        return jnp.sum(lax.all_gather(partial_sum.astype(jnp.bfloat16), "row"), axis=0).astype(
+            jnp.float32
+        )
 
     def col_total(partial_sum):
         return lax.psum(partial_sum.astype(jnp.bfloat16), "col").astype(jnp.float32)

time: 420 us -> 482 us (1.15)
  waiting for transfers between devices: 328 us -> 380 us
  other arithmetic: 2.65 us -> 12 us
  local copies, waits for them, and re-layouts: 8.26 us -> 17.1 us
  matrix products: 56.1 us -> 50.1 us
    all_gather x0 -> x3, waiting for transfers between devices: none -> 193 us  [row_total(): lax.all_gather(partial_sum.astype(jnp.bfloat16), 'row')]
    psum x2 -> x0, waiting for transfers between devices: 137 us -> none  [row_total(): return lax.psum(partial_sum.astype(jnp.bfloat16), 'row').astype(jnp.float32)]
    reduce_scatter x1, waiting for transfers between devices: 5.5 us -> 20.8 us  [on_device(): lax.psum_scatter(solve_back(forward_zero, back_zero, 0).astype(jnp.bfloat...]
    reduce_scatter x2, waiting for transfers between devices: 49.9 us -> 37 us  [ancestor_share(): lax.psum_scatter(partial_sum.astype(jnp.bfloat16), 'col', scatter_dimensi...]
    psum x1, waiting for transfers between devices: 78.4 us -> 66.5 us  [on_device(): lax.psum(later_two.astype(jnp.bfloat16), 'row').astype(jnp.float32)]
    unnamed x12, local copies, waits for them, and re-layouts: 1.78 us -> 11.7 us
    reduce_sum x0 -> x3, other arithmetic: none -> 9.38 us  [row_total(): jnp.sum(lax.all_gather(partial_sum.astype(jnp.bfloat16), 'row'), axis=0)]
    psum x2, waiting for transfers between devices: 56.6 us -> 62.5 us  [col_total(): return lax.psum(partial_sum.astype(jnp.bfloat16), 'col').astype(jnp.float32)]
  transfers between devices with their start and end apart: 8 -> 9, of which waited for: 8 -> 9; matrix products, arithmetic and copies ran while one was open for 5% -> 9% of each run, Pallas kernels for 0% -> 0%
where the time goes in v1:
time: 482 us; the launch traced here: 481 us
  waiting for transfers between devices  380 us (79%)
  matrix products  50.1 us (10%)
  local copies, waits for them, and re-layouts  17.1 us (4%)
  between operations  14.1 us (3%)
  other arithmetic  12 us (2%)
  blocking collectives  7.22 us (1%)
    all_gather x3, waiting for transfers between devices, row_total(): lax.all_gather(partial_sum.astype(jnp.bfloat16), 'row')  193 us
    psum x1, waiting for transfers between devices, on_device(): lax.psum(later_two.astype(jnp.bfloat16), 'row').astype(jnp.float32)  66.5 us
    psum x2, waiting for transfers between devices, col_total(): return lax.psum(partial_sum.astype(jnp.bfloat16), 'col').astype(jnp.float32)  62.5 us
    reduce_scatter x2, waiting for transfers between devices, ancestor_share(): lax.psum_scatter(partial_sum.astype(jnp.bfloat16), 'col', scatter_dimensi...  37 us
    reduce_scatter x1, waiting for transfers between devices, on_device(): lax.psum_scatter(solve_back(forward_zero, back_zero, 0).astype(jnp.bfloat...  20.8 us
    dot_general x2, matrix products, transpose_product(): lax.dot_general(below[panel_index], flat_values, contract_first, preferre...  13.7 us
    unnamed x12, local copies, waits for them, and re-layouts  11.7 us
  transfers between devices with their start and end apart: 9, of which 9 were waited for; matrix products, arithmetic and copies ran while one was open for 9% of the time, Pallas kernels for 0%

profile of v1, /device:TPU:0, one launch (start us, length us, event | category | flops | bytes accessed | tf_op | source)
XLA Modules:
  0.0 481.3 jit_solution(14294825244280828900)
XLA Ops:
  7.2 4.3 fusion.30
  11.6 75.6 %all-gather.7.cloned.1.call-done = bf16[16384,128]{1,0:T(8,128)(2,1)} async-done(((bf16[2048,128]{1,0:T(8,128)(2,1)}), bf16[16384,128]{1,0:T(8,128)(2,1)}) %all-gather.7.cloned.1.call-update) | async-done | bytes 4194320 | tf_op jit(solution)/shard_map/all_gather | solution.py:21
  87.2 3.1 reduce_sum.36
  90.2 6.6 %fusion.20 = f32[2816,128]{0,1:T(8,128)S(1)} fusion(bf16[2048,128]{1,0:T(8,128)(2,1)S(1)} %reduce_sum.36, bf16[2,2816,2048]{2,1,0:T(8,128)(2,1)} %param.8), kind=kOutput, calls=%fused_computation.22 | convolution fusion | flops 1476395008 | bytes 13500416 | tf_op jit(solution)/shard_map/dot_general | solution.py:65
  99.6 30.9 %all-reduce.4.cloned.1.call-done = bf16[1024,128]{1,0:T(8,128)(2,1)} async-done(((bf16[1024,128]{1,0:T(8,128)(2,1)}), bf16[1024,128]{1,0:T(8,128)(2,1)}) %all-reduce.4.cloned.1.call-update) | async-done | bytes 262160 | tf_op jit(solution)/shard_map/psum | solution.py:26
  130.5 4.7 fusion.42
  135.3 7.2 %all_gather.23 = bf16[3072,128]{1,0:T(8,128)(2,1)S(1)} all-gather(bf16[768,128]{1,0:T(8,128)(2,1)S(1)} %copy-done.2), channel_id=1, replica_groups=mesh['row'=8,'col'=4] {'col'}, dimensions={0}, use_global_device_ids=true | all-gather | bytes 983040 | tf_op jit(solution)/shard_map/all_gather | solution.py:86
  143.4 7.0 %fusion.45 = bf16[2048,128]{0,1:T(8,128)(2,1)} fusion(bf16[2816,128]{1,0:T(8,128)(2,1)S(1)} %bitcast.134, bf16[2,2816,2048]{2,1,0:T(8,128)(2,1)} %param.8), kind=kOutput, calls=%fused_computation.33 | convolution fusion | flops 1476657152 | bytes 12779520 | tf_op jit(solution)/shard_map/dot_general | solution.py:52
  150.6 57.6 %all-gather.9.cloned.1.call-done = bf16[16384,128]{0,1:T(8,128)(2,1)} async-done(((bf16[2048,128]{0,1:T(8,128)(2,1)}), bf16[16384,128]{0,1:T(8,128)(2,1)}) %all-gather.9.cloned.1.call-update) | async-done | bytes 4194320 | tf_op jit(solution)/shard_map/all_gather | solution.py:21
  208.1 5.0 %copy.68 = bf16[16,8,8,2048]{3,2,1,0:T(8,128)(2,1)S(1)} copy(bf16[16,8,8,2048]{3,1,2,0:T(8,128)(2,1)} %bitcast.129) | data formatting | bytes 8388608
  213.1 3.2 bitcast_reduce_fusion.1
  216.3 66.5 %all-reduce.6.cloned.1.call-done = bf16[2048,128]{0,1:T(8,128)(2,1)} async-done(((bf16[2048,128]{0,1:T(8,128)(2,1)}), bf16[2048,128]{0,1:T(8,128)(2,1)}) %all-reduce.6.cloned.1.call-update) | async-done | bytes 524304 | tf_op jit(solution)/shard_map/psum | solution.py:91
  282.8 3.8 fusion.72
  286.6 31.6 %all-reduce.8.cloned.1.call-done = bf16[1024,128]{0,1:T(8,128)(2,1)} async-done(((bf16[1024,128]{0,1:T(8,128)(2,1)}), bf16[1024,128]{0,1:T(8,128)(2,1)}) %all-reduce.8.cloned.1.call-update) | async-done | bytes 262160 | tf_op jit(solution)/shard_map/psum | solution.py:26
  320.8 6.8 %fusion.48 = bf16[2048,128]{0,1:T(8,128)(2,1)} fusion(bf16[2816,128]{1,0:T(8,128)(2,1)S(1)} %bitcast.135, bf16[2,2816,2048]{2,1,0:T(8,128)(2,1)} %param.8), kind=kOutput, calls=%fused_computation.34 | convolution fusion | flops 1476657152 | bytes 12779520 | tf_op jit(solution)/shard_map/dot_general | solution.py:52
  330.6 6.7 %fusion.23 = f32[2816,128]{0,1:T(8,128)S(1)} fusion(bf16[2048,128]{0,1:T(8,128)(2,1)} %copy-done, bf16[2,2816,2048]{2,1,0:T(8,128)(2,1)} %param.8), kind=kOutput, calls=%fused_computation.23 | convolution fusion | flops 1476395008 | bytes 13500416 | tf_op jit(solution)/shard_map/dot_general | solution.py:74
  340.6 59.9 %all-gather.11.cloned.1.call-done = bf16[16384,128]{0,1:T(8,128)(2,1)} async-done(((bf16[2048,128]{0,1:T(8,128)(2,1)}), bf16[16384,128]{0,1:T(8,128)(2,1)}) %all-gather.11.cloned.1.call-update) | async-done | bytes 4194320 | tf_op jit(solution)/shard_map/all_gather | solution.py:21
  400.5 5.0 %copy.70 = bf16[16,8,8,2048]{3,2,1,0:T(8,128)(2,1)S(1)} copy(bf16[16,8,8,2048]{3,1,2,0:T(8,128)(2,1)} %bitcast.128) | data formatting | bytes 8388608
  405.5 3.2 bitcast_reduce_fusion
  408.9 3.7 fusion.75
  413.5 11.3 %reduce-scatter.6.cloned.1.call-done = bf16[768,128]{1,0:T(8,128)(2,1)} async-done(((bf16[3072,128]{1,0:T(8,128)(2,1)}), bf16[768,128]{1,0:T(8,128)(2,1)}) %reduce-scatter.6.cloned.1.call-update) | async-done | bytes 196624 | tf_op jit(solution)/shard_map/reduce_scatter | solution.py:80
  424.8 25.8 %reduce-scatter.8.cloned.1.call-done = bf16[768,128]{1,0:T(8,128)(2,1)} async-done(((bf16[3072,128]{1,0:T(8,128)(2,1)}), bf16[768,128]{1,0:T(8,128)(2,1)}) %reduce-scatter.8.cloned.1.call-update) | async-done | bytes 196624 | tf_op jit(solution)/shard_map/reduce_scatter | solution.py:80
  450.6 1.8 subtract_convert_fusion.4
  452.3 20.8 %reduce-scatter.4.cloned.1.call-done = bf16[256,128]{0,1:T(8,128)(2,1)} async-done(((bf16[1024,128]{0,1:T(8,128)(2,1)}), bf16[256,128]{0,1:T(8,128)(2,1)}) %reduce-scatter.4.cloned.1.call-update) | async-done | bytes 65552 | tf_op jit(solution)/shard_map/reduce_scatter | solution.py:96
  (47 shorter events, 15.5 us)
Async XLA Ops:
  7.2 4.4 copy-start.3
  7.2 80.0 %all-gather.7.cloned.1.call-start = ((), (), s32[]{:S(2)}) async-start(), calls=%async_computation.9 | async-start | bytes 4718592 | tf_op jit(solution)/shard_map/all_gather | solution.py:21
  11.5 119.0 %all-reduce.4.cloned.1.call-start = ((), (), s32[]{:S(2)}) async-start(), calls=%async_computation.3 | async-start | bytes 524288 | tf_op jit(solution)/shard_map/psum | solution.py:26
  98.7 36.5 %copy-start.2 = (bf16[768,128]{1,0:T(8,128)(2,1)S(1)}, bf16[768,128]{1,0:T(8,128)(2,1)}, u32[]{:S(2)}) copy-start(bf16[768,128]{1,0:T(8,128)(2,1)} %param.11) | copy-start | bytes 589828
  99.5 108.6 %all-gather.9.cloned.1.call-start = ((), (), s32[]{:S(2)}) async-start(), calls=%async_computation.10 | async-start | bytes 4718592 | tf_op jit(solution)/shard_map/all_gather | solution.py:21
  135.2 147.6 %all-reduce.6.cloned.1.call-start = ((), (), s32[]{:S(2)}) async-start(), calls=%async_computation.4 | async-start | bytes 1048576 | tf_op jit(solution)/shard_map/psum | solution.py:91
  150.4 167.9 %all-reduce.8.cloned.1.call-start = ((), (), s32[]{:S(2)}) async-start(), calls=%async_computation.5 | async-start | bytes 524288 | tf_op jit(solution)/shard_map/psum | solution.py:26
  216.3 101.9 %copy-start = (bf16[2048,128]{0,1:T(8,128)(2,1)}, bf16[2048,128]{0,1:T(8,128)(2,1)S(1)}, u32[]{:S(2)}) copy-start(bf16[2048,128]{0,1:T(8,128)(2,1)S(1)} %bitcast_reduce_fusion.1) | copy-start | bytes 1572868
  286.6 113.9 %all-gather.11.cloned.1.call-start = ((), (), s32[]{:S(2)}) async-start(), calls=%async_computation.11 | async-start | bytes 4718592 | tf_op jit(solution)/shard_map/all_gather | solution.py:21
  327.6 97.2 %reduce-scatter.6.cloned.1.call-start = ((), (), s32[]{:S(2)}) async-start(), calls=%async_computation.7 | async-start | bytes 983040 | tf_op jit(solution)/shard_map/reduce_scatter | solution.py:80
  330.3 120.2 %reduce-scatter.8.cloned.1.call-start = ((), (), s32[]{:S(2)}) async-start(), calls=%async_computation.8 | async-start | bytes 983040 | tf_op jit(solution)/shard_map/reduce_scatter | solution.py:80
  340.5 132.6 %reduce-scatter.4.cloned.1.call-start = ((), (), s32[]{:S(2)}) async-start(), calls=%async_computation.6 | async-start | bytes 327680 | tf_op jit(solution)/shard_map/reduce_scatter | solution.py:96
  408.6 41.9 %copy-start.1 = (bf16[768,128]{1,0:T(8,128)(2,1)S(1)}, bf16[768,128]{1,0:T(8,128)(2,1)}, u32[]{:S(2)}) copy-start(bf16[768,128]{1,0:T(8,128)(2,1)} %param.10) | copy-start | bytes 589828
Sparse Core Ops, SparseCore 0:
  11.6 75.4 all-gather.6
  99.6 30.8 all-reduce.3
  135.3 72.7 all-gather.8
  211.4 71.3 all-reduce.5
  286.7 31.4 all-reduce.7
  327.7 72.7 all-gather.10
  403.0 21.7 reduce-scatter.5
  427.3 23.1 reduce-scatter.7
  453.0 20.0 reduce-scatter.3
